TPU v7x, 32 devices: a whole 2x2x4 slice. The times are simulated.
32 devices in a mesh: row: 8 (over z, x), col: 4 (over y, core).
Axes of the slice: x: 2, y: 2, z: 4, core: 2. Of those that a mesh axis runs over, the one named last changes fastest.
Arguments:
- features: bfloat16 [32768, 256], P(('col', 'row')), may hold values from -6 to 6
- adjacency: bfloat16 [256, 4, 12, 128, 128], P('row', 'col'), may hold values from 0 to 0.023925781
- block_cols: int32 [256, 4, 12], P('row', 'col'), may hold values from 0 to 63, as said below
- block_live: int32 [256, 4], P('row', 'col'), may hold values from 1 to 12, as said below
- weight: bfloat16 [256, 256], replicated, may hold values from -0.375 to 0.375
- bias: float32 [256], replicated, may hold values from -3 to 3
- upstream: bfloat16 [32768, 256], P(('row', 'col')), may hold values from -6 to 6
Outputs:
- activations: bfloat16 [32768, 256], P(('row', 'col'))
- feature_grad: bfloat16 [32768, 256], P(('col', 'row'))
- weight_grad: float32 [256, 256], replicated
- bias_grad: float32 [256], replicated
Inputs may be any that keep to these rules, and one draw needn't show every extreme that they name: `block_cols`: the live slots of one block row in one column tile name distinct column blocks of that tile. Slots k with k < block_live[i, c] are live; the other slots of block_cols and adjacency are ignored. Some entry equals 12.
All inputs are finite; a program needn't handle non-finite values.
Results may differ from a plain program's by a relative error of at most 0.014.
Values may be sent and summed in bfloat16 or wider, within the bound.
No kernel may reach another device: no remote copies, remote signals or barrier semaphores. Data moves between devices by JAX's collectives and lax.ppermute only.
A program may use at most 256 MiB of HBM per device.

v0:
```python
import jax
import jax.numpy as jnp
from jax import lax
from jax.sharding import PartitionSpec as P


def local(features, adjacency, block_cols, block_live, weight, bias, upstream):
    block_rows = adjacency.shape[0]
    block_slots = adjacency.shape[2]
    block_size = adjacency.shape[3]
    feature_width = features.shape[1]
    tile_blocks = adjacency.reshape(block_rows, block_slots, block_size, block_size)
    column_ids = block_cols.reshape(block_rows, block_slots)
    live_count = block_live.reshape(block_rows)
    live_mask = lax.broadcasted_iota(jnp.int32, (block_rows, block_slots), 1) < live_count[:, None]
    feature_panel = lax.all_gather(features, "row", axis=0, tiled=True)
    panel_blocks = feature_panel.shape[0] // block_size
    picked = feature_panel.reshape(panel_blocks, block_size, feature_width)[column_ids]
    picked = jnp.where(live_mask[:, :, None, None], picked, jnp.zeros((), jnp.bfloat16))
    partial_value = jnp.einsum(
        "ikab,ikbf->iaf", tile_blocks, picked, preferred_element_type=jnp.float32
    )
    partial_value = partial_value.reshape(block_rows * block_size, feature_width)
    aggregated = lax.psum_scatter(partial_value, "col", scatter_dimension=0, tiled=True).astype(
        jnp.bfloat16
    )
    preact = jnp.dot(aggregated, weight, preferred_element_type=jnp.float32) + bias
    sigmoid_pre = jax.nn.sigmoid(preact)
    outputs_here = (preact * sigmoid_pre).astype(jnp.bfloat16)
    derivative = sigmoid_pre * (1.0 + preact * (1.0 - sigmoid_pre))
    grad_pre = (upstream.astype(jnp.float32) * derivative).astype(jnp.bfloat16)
    weight_part = jnp.einsum("nf,ng->fg", aggregated, grad_pre, preferred_element_type=jnp.float32)
    bias_part = jnp.sum(grad_pre.astype(jnp.float32), axis=0)
    grad_agg = jnp.einsum("ng,fg->nf", grad_pre, weight, preferred_element_type=jnp.float32).astype(
        jnp.bfloat16
    )
    weight_grad, bias_grad = lax.psum((weight_part, bias_part), ("row", "col"))
    tile_grad = lax.all_gather(grad_agg, "col", axis=0, tiled=True)
    contrib = jnp.einsum(
        "ikab,iaf->ikbf",
        tile_blocks,
        tile_grad.reshape(block_rows, block_size, feature_width),
        preferred_element_type=jnp.float32,
    )
    contrib = contrib.reshape(block_rows * block_slots, block_size, feature_width)
    target_blocks = jnp.where(live_mask, column_ids, panel_blocks).reshape(-1)
    panel_sum = jnp.zeros((panel_blocks, block_size, feature_width), jnp.float32)
    panel_sum = panel_sum.at[target_blocks].add(contrib, mode="drop")
    panel_sum = panel_sum.reshape(panel_blocks * block_size, feature_width)
    feature_grad = lax.psum_scatter(
        panel_sum.astype(jnp.bfloat16), "row", scatter_dimension=0, tiled=True
    )
    return (outputs_here, feature_grad, weight_grad, bias_grad)


def solution(mesh):
    placed = (
        P(("col", "row"), None),
        P("row", "col", None, None, None),
        P("row", "col", None),
        P("row", "col"),
        P(),
        P(),
        P(("row", "col"), None),
    )
    return jax.shard_map(
        local,
        mesh=mesh,
        in_specs=placed,
        out_specs=(P(("row", "col"), None), P(("col", "row"), None), P(), P()),
        check_vma=False,
    )
```

profile of v0, /device:TPU:0, one launch (start us, length us, event | category | flops | bytes accessed | tf_op | source)
XLA Modules:
  0.0 477.6 jit_solution(3709703805803400464)
XLA Ops:
  7.2 0.0 copy-start
  7.2 0.0 all-gather.3.cloned.1.call-start
  7.2 0.7 all-gather.3.cloned.1.call-update
  7.9 0.0 reduce-scatter.3.cloned.1.call-start
  8.0 0.7 compare_select_fusion
  8.7 0.1 copy.12
  8.8 0.1 reshape.129
  8.9 0.7 iota_compare_fusion
  9.6 76.1 %all-gather.3.cloned.1.call-done = bf16[8192,256]{1,0:T(8,128)(2,1)} async-done(((bf16[1024,256]{1,0:T(8,128)(2,1)}), bf16[8192,256]{1,0:T(8,128)(2,1)}) %all-gather.3.cloned.1.call-update) | async-done | bytes 4194320 | tf_op jit(solution)/shard_map/all_gather | solution.py:16
  85.7 15.1 %gather_fusion = bf16[384,128,256]{2,1,0:T(8,128)(2,1)} fusion(bf16[64,128,256]{2,1,0:T(8,128)(2,1)} %bitcast.35, s32[1024]{0:T(1024)S(1)} %pad_clamp_fusion), kind=kCustom, calls=%fused_computation | custom fusion | bytes 50333184 | tf_op jit(solution)/shard_map/gather | solution.py:18
  100.8 0.0 copy-start.3
  100.8 0.0 copy-start.4
  100.8 16.1 %fusion = f32[32,256,128,1]{1,2,3,0:T(8,128)} fusion(bf16[32,12,128,256]{3,2,1,0:T(8,128)(2,1)} %bitcast.36, pred[32,12]{1,0:T(8,128)(4,1)S(1)} %iota_compare_fusion, bf16[32,1,12,128,128]{4,3,2,1,0:T(8,128)(2,1)} %param.8), kind=kOutput, calls=%fused_computation.2 | convolution fusion | flops 3233808384 | bytes 41943424 | tf_op jit(solution)/shard_map/ikab,ikbf->iaf/dot_general | solution.py:20
  116.9 0.0 copy-start.2
  116.9 0.0 reduce-scatter.3.cloned.1.call-update
  116.9 0.0 all-gather.5.cloned.1.call-start
  117.0 43.2 %reduce-scatter.3.cloned.1.call-done = f32[1024,256]{1,0:T(8,128)} async-done(((f32[4096,256]{1,0:T(8,128)}), f32[1024,256]{1,0:T(8,128)}) %reduce-scatter.3.cloned.1.call-update) | async-done | bytes 1048592 | tf_op jit(solution)/shard_map/reduce_scatter | solution.py:24
  160.2 0.0 copy-done
  160.2 0.0 copy-done.3
  160.2 0.0 copy-done.4
  160.2 2.7 convert_reduce_fusion
  162.9 1.1 convolution_convert_fusion
  164.0 0.0 all-gather.5.cloned.1.call-update
  164.0 0.0 all-reduce.2.cloned.1.call-start
  164.1 0.1 lt.53
  164.2 0.0 copy-done.2
  164.2 0.1 copy.13
  164.3 0.1 reshape.124
  164.4 2.3 fusion.7
  166.7 0.0 all-reduce.2.cloned.1.call-update
  166.7 0.0 reduce-scatter.5.cloned.1.call-start
  166.8 20.0 %all-gather.5.cloned.1.call-done = bf16[4096,256]{1,0:T(8,128)(2,1)} async-done(((bf16[1024,256]{1,0:T(8,128)(2,1)}), bf16[4096,256]{1,0:T(8,128)(2,1)}) %all-gather.5.cloned.1.call-update) | async-done | bytes 2097168 | tf_op jit(solution)/shard_map/all_gather | solution.py:38
  186.8 22.5 %fusion.3 = f32[32,256,12,128]{3,1,2,0:T(8,128)} fusion(bf16[32,128,256,1]{2,1,3,0:T(8,128)(2,1)} %bitcast.39, bf16[32,1,12,128,128]{4,3,2,1,0:T(8,128)(2,1)} %param.8), kind=kOutput, calls=%fused_computation.5 | convolution fusion | flops 3221225472 | bytes 65011712 | tf_op jit(solution)/shard_map/ikab,iaf->ikbf/dot_general | solution.py:39
  209.3 48.9 %copy.15 = f32[384,128,256]{2,1,0:T(8,128)} copy(f32[384,128,256]{1,2,0:T(8,128)} %bitcast.34) | data formatting | bytes 100663296 | tf_op jit(solution)/shard_map/reshape | solution.py:45
  258.2 4.2 broadcast_in_dim.23
  262.4 0.0 copy-start.1
  262.4 109.9 %scatter_fusion = f32[64,128,256]{2,1,0:T(8,128)} fusion(f32[64,128,256]{2,1,0:T(8,128)} %broadcast_in_dim.23, s32[384]{0:T(512)S(1)} %fusion.10, f32[384,128,256]{2,1,0:T(8,128)} %copy.15), kind=kCustom, calls=%fused_computation.1 | custom fusion | flops 12582912 | bytes 150996480 | tf_op jit(solution)/shard_map/scatter-add | solution.py:48
  372.3 5.9 %convert_element_type.29 = bf16[64,128,256]{2,1,0:T(8,128)(2,1)} convert(f32[64,128,256]{2,1,0:T(8,128)} %scatter_fusion) | non-fusion elementwise | flops 2097152 | bytes 12582912 | tf_op jit(solution)/shard_map/convert_element_type | solution.py:51
  378.3 0.0 reduce-scatter.5.cloned.1.call-update
  378.3 42.9 %psum.15 = f32[256]{0:T(256)} all-reduce(f32[256]{0:T(256)S(1)} %get-tuple-element.4), channel_id=1, replica_groups=mesh['row'=8,'col'=4] {'row','col'}, use_global_device_ids=true, to_apply=%region_5.6 | all-reduce | flops 256 | bytes 2048 | tf_op jit(solution)/shard_map/psum | solution.py:37
  421.2 0.0 all-reduce.2.cloned.1.call-done
  421.2 48.2 %reduce-scatter.5.cloned.1.call-done = bf16[1024,256]{1,0:T(8,128)(2,1)} async-done(((bf16[8192,256]{1,0:T(8,128)(2,1)}), bf16[1024,256]{1,0:T(8,128)(2,1)}) %reduce-scatter.5.cloned.1.call-update) | async-done | bytes 524304 | tf_op jit(solution)/shard_map/reduce_scatter | solution.py:50
  469.4 1.7 copy.22
  471.1 0.0 copy-done.1
  (2 shorter events, 0.0 us)
Async XLA Ops:
  7.2 153.0 %copy-start = (bf16[256,256]{1,0:T(8,128)(2,1)S(1)}, bf16[256,256]{1,0:T(8,128)(2,1)}, u32[]{:S(2)}) copy-start(bf16[256,256]{1,0:T(8,128)(2,1)} %param.11) | copy-start | bytes 393220
  7.2 78.5 %all-gather.3.cloned.1.call-start = ((), (), s32[]{:S(2)}) async-start(), calls=%async_computation.2 | async-start | bytes 4718592 | tf_op jit(solution)/shard_map/all_gather | solution.py:16
  7.9 152.3 %reduce-scatter.3.cloned.1.call-start = ((), (), s32[]{:S(2)}) async-start(), calls=%async_computation.3 | async-start | bytes 5242880 | tf_op jit(solution)/shard_map/reduce_scatter | solution.py:24
  100.8 59.4 %copy-start.3 = (bf16[1024,256]{1,0:T(8,128)(2,1)S(1)}, bf16[1024,256]{1,0:T(8,128)(2,1)}, u32[]{:S(2)}) copy-start(bf16[1024,256]{1,0:T(8,128)(2,1)} %param.13) | copy-start | bytes 1572868
  100.8 59.4 %copy-start.4 = (f32[256]{0:T(256)S(1)}, f32[256]{0:T(256)}, u32[]{:S(2)}) copy-start(f32[256]{0:T(256)} %param.12) | copy-start | bytes 3076
  116.9 47.3 %copy-start.2 = (s32[32,1,12]{0,1,2:T(1,128)S(1)}, s32[32,1,12]{0,1,2:T(1,128)}, u32[]{:S(2)}) copy-start(s32[32,1,12]{0,1,2:T(1,128)} %param.9) | copy-start | bytes 4612
  116.9 69.9 %all-gather.5.cloned.1.call-start = ((), (), s32[]{:S(2)}) async-start(), calls=%async_computation.4 | async-start | bytes 2621440 | tf_op jit(solution)/shard_map/all_gather | solution.py:38
  164.0 257.2 %all-reduce.2.cloned.1.call-start = ((), (), s32[]{:S(2)}) async-start(), calls=%async_computation.6 | async-start | bytes 524288 | tf_op jit(solution)/shard_map/psum | solution.py:37
  166.7 302.7 %reduce-scatter.5.cloned.1.call-start = ((), (), s32[]{:S(2)}) async-start(), calls=%async_computation.5 | async-start | bytes 4718592 | tf_op jit(solution)/shard_map/reduce_scatter | solution.py:50
  262.4 208.7 %copy-start.1 = (bf16[256,256]{1,0:T(8,128)(2,1)S(1)}, bf16[256,256]{1,0:T(8,128)(2,1)}, u32[]{:S(2)}) copy-start(bf16[256,256]{1,0:T(8,128)(2,1)} %param.11) | copy-start | bytes 393220
Sparse Core Ops, SparseCore 0:
  10.1 75.4 all-gather.2
  117.0 43.1 reduce-scatter.2
  164.2 22.5 all-gather.4
  192.7 126.5 all-reduce.1
  378.4 90.9 reduce-scatter.4
where the time goes:
time: 479 us; the launch traced here: 478 us
  waiting for transfers between devices  188 us (39%)
  other arithmetic  117 us (24%)
  local copies, waits for them, and re-layouts  70.5 us (15%)
  matrix products  44.7 us (9%)
  blocking collectives  42.9 us (9%)
  between operations  13.8 us (3%)
    scatter-add x1, other arithmetic, local(): panel_sum = panel_sum.at[target_blocks].add(contrib, mode='drop')  110 us
    all_gather x1, waiting for transfers between devices, local(): feature_panel = lax.all_gather(features, 'row', axis=0, tiled=True)  76.1 us
    reshape x1, local copies, waits for them, and re-layouts, local(): contrib.reshape(block_rows * block_slots, block_size, feature_width)  48.9 us
    reduce_scatter x1, waiting for transfers between devices, local(): lax.psum_scatter(panel_sum.astype(jnp.bfloat16), 'row', scatter_dimension...  48.2 us
    reduce_scatter x1, waiting for transfers between devices, local(): lax.psum_scatter(partial_value, 'col', scatter_dimension=0, tiled=True)  43.2 us
    psum x1, blocking collectives, local(): weight_grad, bias_grad = lax.psum((weight_part, bias_part), ('row', 'col'))  42.9 us
    dot_general x1, matrix products, local(): jnp.einsum('ikab,iaf->ikbf', tile_blocks, tile_grad.reshape(block_rows, b...  22.5 us
    all_gather x1, waiting for transfers between devices, local(): tile_grad = lax.all_gather(grad_agg, 'col', axis=0, tiled=True)  20 us
  transfers between devices with their start and end apart: 5, of which 4 were waited for; matrix products, arithmetic and copies ran while one was open for 41% of the time, Pallas kernels for 0%

commit v1 on v0

v1 whole, which is shorter than its diff:
```python
import functools

import jax
import jax.numpy as jnp
from jax import lax
from jax.experimental import pallas as pl
from jax.experimental.pallas import tpu as pltpu
from jax.sharding import PartitionSpec as P


F32 = jnp.float32
BF16 = jnp.bfloat16
I32 = jnp.int32
GROUP = 4


def split_row(n_row):
    nx = 1
    while (2 * nx) ** 2 <= n_row and n_row % (2 * nx) == 0:
        nx *= 2
    return n_row // nx, nx


def split_col(n_col):
    nc = 2 if n_col % 2 == 0 else 1
    return n_col // nc, nc


def shift_major(major, minor, step):
    return [
        (a * minor + b, ((a + step) % major) * minor + b)
        for a in range(major)
        for b in range(minor)
    ]


def shift_minor(major, minor, step):
    return [
        (a * minor + b, a * minor + (b + step) % minor)
        for a in range(major)
        for b in range(minor)
    ]


def as_blocks(ref, bs):
    value = ref[...]
    return value.reshape(value.shape[0] // bs, bs, value.shape[1])


def fill_panel(panel, pieces, bs):
    at = 0
    for piece in pieces:
        blocks = as_blocks(piece, bs)
        panel[at : at + blocks.shape[0]] = blocks
        at += blocks.shape[0]
    panel[at] = jnp.zeros(panel.shape[1:], panel.dtype)


def block_rows_at(index, bs):
    return pl.ds(pl.multiple_of(index * bs, bs), bs)


def early_kernel(slots, n_pieces, rows_ref, index_ref, mats, *refs):
    pieces = refs[:n_pieces]
    away_ref, kept_ref, panel = refs[n_pieces:]
    bs = mats.shape[-1]
    fill_panel(panel, pieces, bs)
    half = away_ref.shape[0] // bs
    for part, out_ref in enumerate((away_ref, kept_ref)):

        @pl.loop(0, half // 2)
        def _(pair, part=part, out_ref=out_ref):
            for r in range(2):
                at = pair * 2 + r
                row = rows_ref[part * half + at]
                first = row * slots
                lhs = [mats[first + k] for k in range(slots)]
                rhs = [panel[index_ref[first + k]] for k in range(slots)]
                out_ref[block_rows_at(at, bs), :] = jnp.dot(
                    jnp.concatenate(lhs, axis=1),
                    jnp.concatenate(rhs, axis=0),
                    preferred_element_type=F32,
                )


def cost(flops, moved):
    return pl.CostEstimate(flops=flops, bytes_accessed=moved, transcendentals=0)


SMEM_SPEC = pl.BlockSpec(memory_space=pltpu.SMEM)
VMEM_SPEC = pl.BlockSpec(memory_space=pltpu.VMEM)


def early_product(mats, pieces, rows, index, slots):
    n_mats, bs, _ = mats.shape
    n_rows = n_mats // slots
    width = pieces[0].shape[1]
    bps = pieces[0].shape[0] // bs
    out = jax.ShapeDtypeStruct((n_rows // 2 * bs, width), F32)
    return pl.pallas_call(
        functools.partial(early_kernel, slots, len(pieces)),
        name="early",
        out_shape=(out, out),
        in_specs=[SMEM_SPEC] * 2 + [VMEM_SPEC] * (1 + len(pieces)),
        out_specs=(VMEM_SPEC, VMEM_SPEC),
        scratch_shapes=[pltpu.VMEM((len(pieces) * bps + 1, bs, width), BF16)],
        compiler_params=pltpu.CompilerParams(vmem_limit_bytes=24 << 20),
        cost_estimate=cost(2 * n_mats * bs * bs * width, 20 << 20),
    )(rows, index, mats, *pieces)


def late_kernel(slots, part, rows_ref, count_ref, entry_ref, source_ref, mats, piece, acc_ref, out_ref, panel):
    bs = mats.shape[-1]
    fill_panel(panel, [piece], bs)
    half = out_ref.shape[0] // bs

    def term(row, g):
        at = row * (slots + 2) + 2 * g
        lhs = [mats[entry_ref[at + k]] for k in range(2)]
        rhs = [panel[source_ref[at + k]] for k in range(2)]
        return jnp.dot(
            jnp.concatenate(lhs, axis=1),
            jnp.concatenate(rhs, axis=0),
            preferred_element_type=F32,
        )

    @pl.loop(0, half // 2)
    def _(pair):
        places = [pair * 2 + r for r in range(2)]
        rows = [rows_ref[part * half + at] for at in places]
        accs = tuple(
            acc_ref[block_rows_at(at, bs), :] + term(row, 0)
            for at, row in zip(places, rows, strict=True)
        )
        for r in range(2):

            def more(g, acc, r=r):
                return acc + term(rows[r], g)

            acc = lax.fori_loop(1, (count_ref[rows[r]] + 1) // 2, more, accs[r])
            out_ref[block_rows_at(places[r], bs), :] = acc.astype(BF16)


def late_product(mats, piece, acc, rows, count, entry, source, slots, part):
    bs = mats.shape[1]
    width = piece.shape[1]
    bps = piece.shape[0] // bs
    return pl.pallas_call(
        functools.partial(late_kernel, slots, part),
        name="late",
        out_shape=jax.ShapeDtypeStruct(acc.shape, BF16),
        in_specs=[SMEM_SPEC] * 4 + [VMEM_SPEC] * 3,
        out_specs=VMEM_SPEC,
        scratch_shapes=[pltpu.VMEM((bps + 1, bs, width), BF16)],
        compiler_params=pltpu.CompilerParams(vmem_limit_bytes=20 << 20),
        cost_estimate=cost(acc.size * bs, 4 << 20),
    )(rows, count, entry, source, mats, piece, acc)


def lists_kernel(
    slots, n_rows, n_blocks, n_list, late_from, bps,
    cols_ref, live_ref, place_ref,
    count_ref, entry_ref, source_ref, late_count_ref, late_entry_ref, late_source_ref,
):
    @pl.loop(0, n_blocks)
    def _(b):
        count_ref[b] = 0

    @pl.loop(0, n_rows)
    def _(row):
        place = place_ref[row]

        def visit(k, late):
            at = row * slots + k
            b = cols_ref[at]
            n = count_ref[b]
            entry_ref[b * n_list + n] = at
            source_ref[b * n_list + n] = place
            count_ref[b] = n + 1
            late_entry_ref[row * (slots + 2) + late] = at
            late_source_ref[row * (slots + 2) + late] = jnp.maximum(b - late_from, 0)
            return late + (b >= late_from).astype(I32)

        late = lax.fori_loop(0, live_ref[row], visit, jnp.int32(0))
        late_count_ref[row] = late
        for k in range(2):
            late_entry_ref[row * (slots + 2) + late + k] = row * slots
            late_source_ref[row * (slots + 2) + late + k] = bps

    @pl.loop(0, n_blocks)
    def _(b):
        n = count_ref[b]
        for k in range(GROUP):
            entry_ref[b * n_list + n + k] = 0
            source_ref[b * n_list + n + k] = n_rows


def slot_lists(cols, live, place, slots, n_blocks, late_from, bps):
    n_rows = live.shape[0]
    n_list = n_rows + GROUP
    sizes = (n_blocks, n_blocks * n_list, n_blocks * n_list, n_rows, n_rows * (slots + 2), n_rows * (slots + 2))
    return pl.pallas_call(
        functools.partial(lists_kernel, slots, n_rows, n_blocks, n_list, late_from, bps),
        name="lists",
        out_shape=tuple(jax.ShapeDtypeStruct((size,), I32) for size in sizes),
        in_specs=[SMEM_SPEC] * 3,
        out_specs=(SMEM_SPEC,) * 6,
        cost_estimate=cost(0, 20 << 20),
    )(cols, live, place)


def backward_kernel(n_list, n_pieces, firsts, bps, count_ref, entry_ref, source_ref, mats, *refs):
    pieces = refs[:n_pieces]
    outs, panel = refs[n_pieces:-1], refs[-1]
    bs = mats.shape[-1]
    fill_panel(panel, pieces, bs)

    def term(b, g):
        at = b * n_list + jnp.minimum(g * GROUP, count_ref[b])
        lhs = [mats[entry_ref[at + k]] for k in range(GROUP)]
        rhs = [panel[source_ref[at + k]] for k in range(GROUP)]
        return lax.dot_general(
            jnp.concatenate(lhs, axis=0),
            jnp.concatenate(rhs, axis=0),
            (((0,), (0,)), ((), ())),
            preferred_element_type=F32,
        )

    for first, out_ref in zip(firsts, outs, strict=True):

        @pl.loop(0, bps // 2)
        def _(pair, first=first, out_ref=out_ref):
            here = [first + 2 * pair + r for r in range(2)]
            most = jnp.maximum(count_ref[here[0]], count_ref[here[1]])
            accs = tuple(term(b, 0) for b in here)

            def more(g, accs):
                return tuple(acc + term(b, g) for b, acc in zip(here, accs, strict=True))

            accs = lax.fori_loop(1, (most + GROUP - 1) // GROUP, more, accs)
            for r in range(2):
                out_ref[block_rows_at(2 * pair + r, bs), :] = accs[r].astype(BF16)


def backward_product(mats, pieces, lists, firsts, bps, slots):
    count, entry, source = lists
    n_mats, bs, _ = mats.shape
    n_rows = n_mats // slots
    width = pieces[0].shape[1]
    out = jax.ShapeDtypeStruct((bps * bs, width), BF16)
    share = n_mats // 8 * len(firsts)
    return pl.pallas_call(
        functools.partial(backward_kernel, n_rows + GROUP, len(pieces), firsts, bps),
        name="backward",
        out_shape=(out,) * len(firsts),
        in_specs=[SMEM_SPEC] * 3 + [VMEM_SPEC] * (1 + len(pieces)),
        out_specs=(VMEM_SPEC,) * len(firsts),
        scratch_shapes=[pltpu.VMEM((n_rows + 1, bs, width), BF16)],
        compiler_params=pltpu.CompilerParams(vmem_limit_bytes=20 << 20),
        cost_estimate=cost(2 * share * bs * bs * width, 4 << 20),
    )(count, entry, source, mats, *pieces)


def local(n_row, n_col, features, adjacency, block_cols, block_live, weight, bias, upstream):
    n_rows, _, slots, bs, _ = adjacency.shape
    width = features.shape[1]
    nz, nx = split_row(n_row)
    ny, nc = split_col(n_col)
    bps = features.shape[0] // bs
    rpc = n_rows // n_col
    me_row, me_col = lax.axis_index("row"), lax.axis_index("col")
    z, x = me_row // nx, me_row % nx
    y, c = me_col // nc, me_col % nc
    to_z = shift_major(nz, nx, 1)
    to_x = shift_minor(nz, nx, 1)
    to_y = shift_major(ny, nc, 1)
    to_c = shift_minor(ny, nc, 1)

    live = block_live.reshape(n_rows)
    cols = block_cols.reshape(n_rows, slots)
    shard = cols // bps
    back_z = (z - shard // nx) % nz
    back_x = (x - shard % nx) % nx
    cols = (back_z * nx + back_x) * bps + cols % bps
    late_from = (n_row - 1) * bps
    is_live = lax.broadcasted_iota(I32, (n_rows, slots), 1) < live[:, None]
    index = jnp.where(is_live, jnp.minimum(cols, late_from), late_from).reshape(-1)
    cols = cols.reshape(-1)
    row_ids = jnp.arange(n_rows, dtype=I32)
    owner = row_ids // rpc
    back_y = (y - owner // nc) % ny
    back_c = (c - owner % nc) % nc
    place = ((back_y * nc + back_c) * rpc + row_ids % rpc).astype(I32)
    order = [(v, u) for u in list(range(1, nc)) + [0] for v in list(range(1, ny)) + [0]]
    dest = jnp.stack([((y - v) % ny) * nc + (c - u) % nc for v, u in order])
    rows = (dest[:, None] * rpc + jnp.arange(rpc, dtype=I32)[None, :]).reshape(-1).astype(I32)
    mats = pltpu.with_memory_space_constraint(
        adjacency.reshape(n_rows * slots, bs, bs), pltpu.VMEM
    )

    pieces = []
    moving = features
    for j in range(nz):
        across = moving
        pieces.append(across)
        for _ in range(1, nx):
            across = lax.ppermute(across, "row", to_x)
            pieces.append(across)
        if j < nz - 1:
            moving = lax.ppermute(moving, "row", to_z)
    *lists, late_count, late_entry, late_source = slot_lists(
        cols, live, place, slots, n_row * bps, late_from, bps
    )
    sums = early_product(mats, pieces[:-1], rows, index, slots)
    halves = []
    for part in range(2):
        halves.append(
            late_product(
                mats, pieces[-1], sums[part], rows, late_count, late_entry, late_source, slots, part
            )
        )
    away, kept = halves
    chunk = rpc * bs
    arrived = lax.ppermute(away, "col", to_c)

    def part_of(value, at):
        return value[at * chunk : (at + 1) * chunk]

    moving = None
    for at in range(ny - 1):
        total = part_of(kept, at).astype(F32) + part_of(arrived, at).astype(F32)
        if moving is not None:
            total = total + moving.astype(F32)
        moving = lax.ppermute(total.astype(BF16), "col", to_y)
    total = part_of(kept, ny - 1).astype(F32) + part_of(arrived, ny - 1).astype(F32)
    if moving is not None:
        total = total + moving.astype(F32)
    aggregated = total.astype(BF16)

    preact = jnp.dot(aggregated, weight, preferred_element_type=F32) + bias
    sigmoid_pre = jax.nn.sigmoid(preact)
    outputs_here = (preact * sigmoid_pre).astype(BF16)
    derivative = sigmoid_pre * (1.0 + preact * (1.0 - sigmoid_pre))
    grad_pre = (upstream.astype(F32) * derivative).astype(BF16)
    grad_agg = jnp.einsum("ng,fg->nf", grad_pre, weight, preferred_element_type=F32).astype(BF16)

    grads = []
    moving = grad_agg
    for v in range(ny):
        across = moving
        grads.append(across)
        for _ in range(1, nc):
            across = lax.ppermute(across, "col", to_c)
            grads.append(across)
        if v < ny - 1:
            moving = lax.ppermute(moving, "col", to_y)

    weight_part = jnp.einsum("nf,ng->fg", aggregated, grad_pre, preferred_element_type=F32)
    bias_part = jnp.sum(grad_pre.astype(F32), axis=0)
    unit = n_col * 8
    packed = jnp.concatenate(
        [weight_part, jnp.broadcast_to(bias_part[None, :], (unit, width))], axis=0
    )
    packed = reduce_small(packed, n_row, n_col)
    weight_grad, bias_grad = packed[:width], packed[width]

    def contribution(j, t):
        return backward_product(mats, grads, lists, ((j * nx + t) * bps,), bps, slots)[0]

    moving = None
    for j in list(range(1, nz)) + [0]:
        across = None
        for t in range(1, nx):
            value = contribution(j, t)
            if across is not None:
                value = (value.astype(F32) + across.astype(F32)).astype(BF16)
            across = lax.ppermute(value, "row", to_x)
        total = contribution(j, 0).astype(F32)
        if across is not None:
            total = total + across.astype(F32)
        if moving is not None:
            total = total + moving.astype(F32)
        total = total.astype(BF16)
        if j:
            moving = lax.ppermute(total, "row", to_z)
    return outputs_here, total, weight_grad, bias_grad


def pick(parts, at):
    return lax.dynamic_index_in_dim(parts, at, 0, keepdims=False)


def reduce_small(packed, n_row, n_col):
    _, width = packed.shape
    ny, nc = split_col(n_col)
    me_col = lax.axis_index("col")
    y, c = me_col // nc, me_col % nc
    to_y, to_c = shift_major(ny, nc, 1), shift_minor(ny, nc, 1)

    def scatter(value, n, me, pairs):
        parts = value.reshape(n, value.shape[0] // n, width)
        moving = pick(parts, (me - 1) % n)
        for s in range(2, n + 1):
            moving = lax.ppermute(moving, "col", pairs) + pick(parts, (me - s) % n)
        return moving

    def gather(value, n, me, pairs):
        out = jnp.zeros((n,) + value.shape, value.dtype)
        for s in range(n):
            out = lax.dynamic_update_index_in_dim(out, value, (me - s) % n, 0)
            if s < n - 1:
                value = lax.ppermute(value, "col", pairs)
        return out.reshape(n * value.shape[0], width)

    total = scatter(packed, nc, c, to_c)
    total = scatter(total, ny, y, to_y)
    step = 1
    while step < n_row:
        other = lax.ppermute(total, "row", [(i, i ^ step) for i in range(n_row)])
        total = total + other
        step *= 2
    total = gather(total, ny, y, to_y)
    return gather(total, nc, c, to_c)


def solution(mesh):
    n_row, n_col = mesh.shape["row"], mesh.shape["col"]
    placed = (
        P(("col", "row"), None),
        P("row", "col", None, None, None),
        P("row", "col", None),
        P("row", "col"),
        P(),
        P(),
        P(("row", "col"), None),
    )

    def body(*args):
        return local(n_row, n_col, *args)

    return jax.shard_map(
        body,
        mesh=mesh,
        in_specs=placed,
        out_specs=(P(("row", "col"), None), P(("col", "row"), None), P(), P()),
        check_vma=False,
    )
```

time: 479 us -> 209 us (0.44)
  other arithmetic: 117 us -> 9.85 us
  waiting for transfers between devices: 188 us -> 102 us
  local copies, waits for them, and re-layouts: 70.5 us -> 27.2 us
  blocking collectives: 42.9 us -> 0 us
  matrix products: 44.7 us -> 2.24 us
  Pallas kernels: 0 us -> 35.5 us
  starting transfers between devices: 0.2 us -> 30.4 us
  between operations: 13.8 us -> 1.06 us
    scatter-add x1 -> x0, other arithmetic: 110 us -> none  [local(): panel_sum = panel_sum.at[target_blocks].add(contrib, mode='drop')]
    ppermute x0 -> x26, waiting for transfers between devices: none -> 102 us  [the longest x3 37.1 us: local(): moving = lax.ppermute(moving, 'row', to_z)]
    all_gather x2 -> x0, waiting for transfers between devices: 96.1 us -> none  [the longest x1 76.1 us: local(): feature_panel = lax.all_gather(features, 'row', axis=0, tiled=True)]
    reduce_scatter x2 -> x0, waiting for transfers between devices: 91.5 us -> none  [the longest x1 48.2 us: local(): lax.psum_scatter(panel_sum.astype(jnp.bfloat16), 'row', scatter_dimension...]
    reshape x2 -> x1, local copies, waits for them, and re-layouts: 49 us -> 0.1 us  [local(): cols = block_cols.reshape(n_rows, slots)]
    psum x1 -> x0, blocking collectives: 42.9 us -> none  [local(): weight_grad, bias_grad = lax.psum((weight_part, bias_part), ('row', 'col'))]
    dot_general x5 -> x3, matrix products: 44.7 us -> 2.24 us  [the longest x1 1.52 us: local(): preact = jnp.dot(aggregated, weight, preferred_element_type=F32) + bias]
    pallas_call x0 -> x12, Pallas kernels: none -> 35.5 us  [the longest x8 17.9 us: backward_product(): pl.pallas_call(functools.partial(backward_kernel, n_rows + GROUP, len(pie...]
  transfers between devices with their start and end apart: 5 -> 26, of which waited for: 4 -> 13; matrix products, arithmetic and copies ran while one was open for 41% -> 5% of each run, Pallas kernels for 0% -> 15%
where the time goes in v1:
time: 209 us; the launch traced here: 208 us
  waiting for transfers between devices  102 us (49%)
  Pallas kernels  35.5 us (17%)
  starting transfers between devices  30.4 us (15%)
  local copies, waits for them, and re-layouts  27.2 us (13%)
  other arithmetic  9.85 us (5%)
  matrix products  2.24 us (1%)
    ppermute x3, waiting for transfers between devices, local(): moving = lax.ppermute(moving, 'row', to_z)  37.1 us
    unnamed x45, local copies, waits for them, and re-layouts  25.6 us
    pallas_call x8, Pallas kernels, backward_product(): pl.pallas_call(functools.partial(backward_kernel, n_rows + GROUP, len(pie...  17.9 us
    ppermute x3, waiting for transfers between devices, reduce_small(): other = lax.ppermute(total, 'row', [(i, i ^ step) for i in range(n_row)])  15.2 us
    ppermute x1, waiting for transfers between devices, local(): moving = lax.ppermute(total.astype(BF16), 'col', to_y)  13 us
    ppermute x1, waiting for transfers between devices, local(): moving = lax.ppermute(moving, 'col', to_y)  12.1 us
    pallas_call x1, Pallas kernels, early_product(): pl.pallas_call(functools.partial(early_kernel, slots, len(pieces)), name=...  8.11 us
    ppermute x4, waiting for transfers between devices, local(): across = lax.ppermute(across, 'row', to_x)  7.69 us
  transfers between devices with their start and end apart: 26, of which 13 were waited for; matrix products, arithmetic and copies ran while one was open for 5% of the time, Pallas kernels for 15%

profile of v1, /device:TPU:0, one launch (start us, length us, event | category | flops | bytes accessed | tf_op | source)
XLA Modules:
  0.0 208.3 jit_solution(12872827936066444128)
XLA Ops:
  0.6 3.1 %collective-permute-start = (bf16[1024,256]{1,0:T(8,128)(2,1)}, bf16[1024,256]{1,0:T(8,128)(2,1)S(1)}, u32[]{:S(2)}, u32[]{:S(2)}) collective-permute-start(bf16[1024,256]{1,0:T(8,128)(2,1)} %refs_0_.1), channel_id=1, source_target_pairs={{0,8},{4,12},{8,16},{12,20},{16,24},{20,28},{24,0},{28,4},{1,9},{5... | collective-permute-start | bytes 1572872 | tf_op jit(solution)/shard_map/ppermute | solution.py:310
  3.8 14.2 %collective-permute-done.refs_2_ = bf16[1024,256]{1,0:T(8,128)(2,1)S(1)} collective-permute-done((bf16[1024,256]{1,0:T(8,128)(2,1)}, bf16[1024,256]{1,0:T(8,128)(2,1)S(1)}, u32[]{:S(2)}, u32[]{:S(2)}) %collective-permute-start) | collective-permute-done | bytes 524320 | tf_op jit(solution)/shard_map/ppermute | solution.py:310
  17.9 1.5 collective-permute-start.4
  19.4 13.4 %collective-permute-done.1.refs_4_ = bf16[1024,256]{1,0:T(8,128)(2,1)S(1)} collective-permute-done((bf16[1024,256]{1,0:T(8,128)(2,1)S(1)}, bf16[1024,256]{1,0:T(8,128)(2,1)S(1)}, u32[]{:S(2)}, u32[]{:S(2)}) %collective-permute-start.1) | collective-permute-done | bytes 524320 | tf_op jit(solution)/shard_map/ppermute | solution.py:310
  34.6 1.3 collective-permute-start.5
  37.3 9.5 %collective-permute-done.2.refs_6_ = bf16[1024,256]{1,0:T(8,128)(2,1)S(1)} collective-permute-done((bf16[1024,256]{1,0:T(8,128)(2,1)S(1)}, bf16[1024,256]{1,0:T(8,128)(2,1)S(1)}, u32[]{:S(2)}, u32[]{:S(2)}) %collective-permute-start.2) | collective-permute-done | bytes 524320 | tf_op jit(solution)/shard_map/ppermute | solution.py:310
  46.8 1.1 collective-permute-start.3
  48.5 4.5 %lists.1 = (s32[64]{0:T(128)}, s32[2304]{0:T(1024)}, s32[2304]{0:T(1024)}, s32[32]{0:T(128)}, s32[448]{0:T(512)}, /*index=5*/s32[448]{0:T(512)}) custom-call(s32[384]{0:T(512)} %get-tuple-element.25.cols_ref, s32[32]{0:T(128)} %bitcast.54, s32[32]{0:T(128)} %fusion.10.place_ref), custom_call_target="tpu_custom_call" | custom-call | bytes 20971520 | tf_op jit(solution)/shard_map/lists/pallas_call | solution.py:202
  53.1 7.7 %collective-permute-done.6.refs_5_ = bf16[1024,256]{1,0:T(8,128)(2,1)} collective-permute-done((bf16[1024,256]{1,0:T(8,128)(2,1)S(1)}, bf16[1024,256]{1,0:T(8,128)(2,1)}, u32[]{:S(2)}, u32[]{:S(2)}) %collective-permute-start.6) | collective-permute-done | bytes 524320 | tf_op jit(solution)/shard_map/ppermute | solution.py:307
  60.8 4.6 %copy-done.1 = bf16[32,1,12,128,128]{4,3,2,1,0:T(8,128)(2,1)S(1)} copy-done((bf16[32,1,12,128,128]{4,3,2,1,0:T(8,128)(2,1)S(1)}, bf16[32,1,12,128,128]{4,3,2,1,0:T(8,128)(2,1)}, u32[]{:S(2)}) %copy-start.1) | copy-done | bytes 12582936
  66.4 8.1 %early.1 = (f32[2048,256]{1,0:T(8,128)S(1)}, f32[2048,256]{1,0:T(8,128)S(1)}) custom-call(s32[32]{0:T(128)S(1)} %add.234.rows_ref, s32[384]{0:T(512)S(1)} %get-tuple-element.24.index_ref, bf16[384,128,128]{2,1,0:T(8,128)(2,1)S(1)} %bitcast.34, bf16[1024,256]{1,0:T(8,128)(2,1)S(1)} %copy-done.9, bf16[1024,256]{1,0:T(8,128)(2,1)S(1)} %collective-permute-done.4.refs_1_, ...), custom_call_target="tpu_custom_call" | custom-call | flops 3221225472 | bytes 20971520 | tf_op jit(solution)/shard_map/early/pallas_call | solution.py:100
  74.6 2.4 %late.3 = bf16[2048,256]{1,0:T(8,128)(2,1)S(1)} custom-call(s32[32]{0:T(128)S(1)} %add.234.rows_ref, s32[32]{0:T(128)S(1)} %copy-done.13, s32[448]{0:T(512)S(1)} %copy-done.11, s32[448]{0:T(512)S(1)} %copy-done.12, bf16[384,128,128]{2,1,0:T(8,128)(2,1)S(1)} %bitcast.35, bf16[1024,256]{1,0:T(8,128)(2,1)S(1)} %collective-permute-done.3.piece, ...), custom_call_target="tpu_custom_call" | custom-call | flops 67108864 | bytes 4194304 | tf_op jit(solution)/shard_map/late/pallas_call | solution.py:148
  77.1 2.6 %late.2 = bf16[2048,256]{1,0:T(8,128)(2,1)S(1)} custom-call(s32[32]{0:T(128)S(1)} %add.234.rows_ref, s32[32]{0:T(128)S(1)} %copy-done.13, s32[448]{0:T(512)S(1)} %copy-done.11, s32[448]{0:T(512)S(1)} %copy-done.12, bf16[384,128,128]{2,1,0:T(8,128)(2,1)S(1)} %bitcast.36, bf16[1024,256]{1,0:T(8,128)(2,1)S(1)} %collective-permute-done.3.piece, ...), custom_call_target="tpu_custom_call" | custom-call | flops 67108864 | bytes 4194304 | tf_op jit(solution)/shard_map/late/pallas_call | solution.py:148
  79.9 1.4 collective-permute-start.8
  81.3 13.0 %collective-permute-done.8 = bf16[1024,256]{1,0:T(8,128)(2,1)S(1)} collective-permute-done((bf16[1024,256]{1,0:T(8,128)(2,1)S(1)}, bf16[1024,256]{1,0:T(8,128)(2,1)S(1)}, u32[]{:S(2)}, u32[]{:S(2)}) %collective-permute-start.8) | collective-permute-done | bytes 524320 | tf_op jit(solution)/shard_map/ppermute | solution.py:334
  94.3 1.5 convert_reduce_fusion
  96.9 1.4 collective-permute-start.10
  98.3 12.1 %collective-permute-done.10.refs_2_ = bf16[1024,256]{1,0:T(8,128)(2,1)S(1)} collective-permute-done((bf16[1024,256]{1,0:T(8,128)(2,1)S(1)}, bf16[1024,256]{1,0:T(8,128)(2,1)S(1)}, u32[]{:S(2)}, u32[]{:S(2)}) %collective-permute-start.10) | collective-permute-done | bytes 524320 | tf_op jit(solution)/shard_map/ppermute | solution.py:356
  110.4 1.9 collective-permute-done.11.refs_3_
  112.3 4.6 %copy-done.3 = bf16[32,1,12,128,128]{4,3,2,1,0:T(8,128)(2,1)S(1)} copy-done((bf16[32,1,12,128,128]{4,3,2,1,0:T(8,128)(2,1)S(1)}, bf16[32,1,12,128,128]{4,3,2,1,0:T(8,128)(2,1)}, u32[]{:S(2)}) %copy-start.3) | copy-done | bytes 12582936
  116.9 2.2 %backward.15 = bf16[1024,256]{1,0:T(8,128)(2,1)S(1)} custom-call(s32[64]{0:T(128)S(1)} %copy-done.10, s32[2304]{0:T(1024)S(1)} %copy-done.7, s32[2304]{0:T(1024)S(1)} %copy-done.8, bf16[384,128,128]{2,1,0:T(8,128)(2,1)S(1)} %bitcast.37, bf16[1024,256]{1,0:T(8,128)(2,1)S(1)} %convolution_convert_fusion.refs_0_, ...), custom_call_target="tpu_custom_call" | custom-call | flops 402653184 | bytes 4194304 | tf_op jit(solution)/shard_map/backward/pallas_call | solution.py:252
  119.1 1.4 collective-permute-start.15
  121.0 2.2 %backward.13 = bf16[1024,256]{1,0:T(8,128)(2,1)S(1)} custom-call(s32[64]{0:T(128)S(1)} %copy-done.10, s32[2304]{0:T(1024)S(1)} %copy-done.7, s32[2304]{0:T(1024)S(1)} %copy-done.8, bf16[384,128,128]{2,1,0:T(8,128)(2,1)S(1)} %bitcast.38, bf16[1024,256]{1,0:T(8,128)(2,1)S(1)} %convolution_convert_fusion.refs_0_, ...), custom_call_target="tpu_custom_call" | custom-call | flops 402653184 | bytes 4194304 | tf_op jit(solution)/shard_map/backward/pallas_call | solution.py:252
  123.2 1.7 collective-permute-start.14
  124.9 2.2 %backward.14 = bf16[1024,256]{1,0:T(8,128)(2,1)S(1)} custom-call(s32[64]{0:T(128)S(1)} %copy-done.10, s32[2304]{0:T(1024)S(1)} %copy-done.7, s32[2304]{0:T(1024)S(1)} %copy-done.8, bf16[384,128,128]{2,1,0:T(8,128)(2,1)S(1)} %bitcast.39, bf16[1024,256]{1,0:T(8,128)(2,1)S(1)} %convolution_convert_fusion.refs_0_, ...), custom_call_target="tpu_custom_call" | custom-call | flops 402653184 | bytes 4194304 | tf_op jit(solution)/shard_map/backward/pallas_call | solution.py:252
  127.1 6.9 %collective-permute-done.15 = bf16[1024,256]{1,0:T(8,128)(2,1)S(1)} collective-permute-done((bf16[1024,256]{1,0:T(8,128)(2,1)S(1)}, bf16[1024,256]{1,0:T(8,128)(2,1)S(1)}, u32[]{:S(2)}, u32[]{:S(2)}) %collective-permute-start.15) | collective-permute-done | bytes 524320 | tf_op jit(solution)/shard_map/ppermute | solution.py:377
  134.9 2.3 %collective-permute-start.20 = (f32[72,256]{1,0:T(8,128)S(1)}, f32[72,256]{1,0:T(8,128)S(1)}, u32[]{:S(2)}, u32[]{:S(2)}) collective-permute-start(f32[72,256]{1,0:T(8,128)S(1)} %dynamic-slice_bitcast_fusion.1), channel_id=1, source_target_pairs={{0,2},{1,3},{2,0},{3,1},{4,6},{5,7},{6,4},{7,5},{8,10},{9,11},{10,... | collective-permute-start | bytes 221192 | tf_op jit(solution)/shard_map/ppermute | solution.py:404
  137.3 2.3 %collective-permute-done.20 = f32[72,256]{1,0:T(8,128)S(1)} collective-permute-done((f32[72,256]{1,0:T(8,128)S(1)}, f32[72,256]{1,0:T(8,128)S(1)}, u32[]{:S(2)}, u32[]{:S(2)}) %collective-permute-start.20) | collective-permute-done | bytes 73760 | tf_op jit(solution)/shard_map/ppermute | solution.py:404
  139.6 1.8 collective-permute-start.21
  141.4 4.6 %copy-done.4 = bf16[32,1,12,128,128]{4,3,2,1,0:T(8,128)(2,1)S(1)} copy-done((bf16[32,1,12,128,128]{4,3,2,1,0:T(8,128)(2,1)S(1)}, bf16[32,1,12,128,128]{4,3,2,1,0:T(8,128)(2,1)}, u32[]{:S(2)}) %copy-start.4) | copy-done | bytes 12582936
  146.0 2.5 %backward.11 = bf16[1024,256]{1,0:T(8,128)(2,1)S(1)} custom-call(s32[64]{0:T(128)S(1)} %copy-done.10, s32[2304]{0:T(1024)S(1)} %copy-done.7, s32[2304]{0:T(1024)S(1)} %copy-done.8, bf16[384,128,128]{2,1,0:T(8,128)(2,1)S(1)} %bitcast.40, bf16[1024,256]{1,0:T(8,128)(2,1)S(1)} %convolution_convert_fusion.refs_0_, ...), custom_call_target="tpu_custom_call" | custom-call | flops 402653184 | bytes 4194304 | tf_op jit(solution)/shard_map/backward/pallas_call | solution.py:252
  149.1 2.2 %backward.12 = bf16[1024,256]{1,0:T(8,128)(2,1)S(1)} custom-call(s32[64]{0:T(128)S(1)} %copy-done.10, s32[2304]{0:T(1024)S(1)} %copy-done.7, s32[2304]{0:T(1024)S(1)} %copy-done.8, bf16[384,128,128]{2,1,0:T(8,128)(2,1)S(1)} %bitcast.41, bf16[1024,256]{1,0:T(8,128)(2,1)S(1)} %convolution_convert_fusion.refs_0_, ...), custom_call_target="tpu_custom_call" | custom-call | flops 402653184 | bytes 4194304 | tf_op jit(solution)/shard_map/backward/pallas_call | solution.py:252
  151.3 2.2 %add_convert_fusion.2 = bf16[1024,256]{1,0:T(8,128)(2,1)} fusion(bf16[1024,256]{1,0:T(8,128)(2,1)} %collective-permute-done.16, bf16[1024,256]{1,0:T(8,128)(2,1)} %collective-permute-done.14, bf16[1024,256]{1,0:T(8,128)(2,1)S(1)} %backward.12), kind=kLoop, calls=%fused_computation.5 | loop fusion | flops 1572864 | bytes 2097152 | tf_op jit(solution)/shard_map/convert_element_type | solution.py:383
  153.5 1.1 collective-permute-start.17
  154.6 4.3 %collective-permute-start.22 = (f32[72,256]{1,0:T(8,128)S(1)}, f32[72,256]{1,0:T(8,128)S(1)}, u32[]{:S(2)}, u32[]{:S(2)}) collective-permute-start(f32[72,256]{1,0:T(8,128)S(1)} %add.270), channel_id=1, source_target_pairs={{0,8},{4,12},{8,0},{12,4},{16,24},{20,28},{24,16},{28,20},{1,9},{5... | collective-permute-start | bytes 221192 | tf_op jit(solution)/shard_map/ppermute | solution.py:419
  159.0 10.1 %collective-permute-done.22 = f32[72,256]{1,0:T(8,128)S(1)} collective-permute-done((f32[72,256]{1,0:T(8,128)S(1)}, f32[72,256]{1,0:T(8,128)S(1)}, u32[]{:S(2)}, u32[]{:S(2)}) %collective-permute-start.22) | collective-permute-done | bytes 73760 | tf_op jit(solution)/shard_map/ppermute | solution.py:419
  169.9 5.1 %collective-permute-done.23 = f32[72,256]{1,0:T(8,128)S(1)} collective-permute-done((f32[72,256]{1,0:T(8,128)S(1)}, f32[72,256]{1,0:T(8,128)S(1)}, u32[]{:S(2)}, u32[]{:S(2)}) %collective-permute-start.23) | collective-permute-done | bytes 73760 | tf_op jit(solution)/shard_map/ppermute | solution.py:419
  175.0 3.6 %collective-permute-start.24 = (f32[72,256]{1,0:T(8,128)S(1)}, f32[72,256]{1,0:T(8,128)S(1)}, u32[]{:S(2)}, u32[]{:S(2)}) collective-permute-start(f32[72,256]{1,0:T(8,128)S(1)} %get-tuple-element.21), channel_id=1, source_target_pairs={{0,2},{1,3},{2,0},{3,1},{4,6},{5,7},{6,4},{7,5},{8,10},{9,11},{10,... | collective-permute-start | bytes 221192 | tf_op jit(solution)/shard_map/ppermute | solution.py:412
  178.7 4.6 %copy-done.5 = bf16[32,1,12,128,128]{4,3,2,1,0:T(8,128)(2,1)S(1)} copy-done((bf16[32,1,12,128,128]{4,3,2,1,0:T(8,128)(2,1)S(1)}, bf16[32,1,12,128,128]{4,3,2,1,0:T(8,128)(2,1)}, u32[]{:S(2)}) %copy-start.5) | copy-done | bytes 12582936
  183.2 2.5 %backward.9 = bf16[1024,256]{1,0:T(8,128)(2,1)S(1)} custom-call(s32[64]{0:T(128)S(1)} %copy-done.10, s32[2304]{0:T(1024)S(1)} %copy-done.7, s32[2304]{0:T(1024)S(1)} %copy-done.8, bf16[384,128,128]{2,1,0:T(8,128)(2,1)S(1)} %bitcast.42, bf16[1024,256]{1,0:T(8,128)(2,1)S(1)} %convolution_convert_fusion.refs_0_, ...), custom_call_target="tpu_custom_call" | custom-call | flops 402653184 | bytes 4194304 | tf_op jit(solution)/shard_map/backward/pallas_call | solution.py:252
  185.7 1.9 collective-permute-start.12
  187.6 2.2 %backward.10 = bf16[1024,256]{1,0:T(8,128)(2,1)S(1)} custom-call(s32[64]{0:T(128)S(1)} %copy-done.10, s32[2304]{0:T(1024)S(1)} %copy-done.7, s32[2304]{0:T(1024)S(1)} %copy-done.8, bf16[384,128,128]{2,1,0:T(8,128)(2,1)S(1)} %bitcast.43, bf16[1024,256]{1,0:T(8,128)(2,1)S(1)} %convolution_convert_fusion.refs_0_, ...), custom_call_target="tpu_custom_call" | custom-call | flops 402653184 | bytes 4194304 | tf_op jit(solution)/shard_map/backward/pallas_call | solution.py:252
  189.8 2.2 %add_convert_fusion.1 = bf16[1024,256]{1,0:T(8,128)(2,1)} fusion(bf16[1024,256]{1,0:T(8,128)(2,1)} %collective-permute-done.17, bf16[1024,256]{1,0:T(8,128)(2,1)} %collective-permute-done.13, bf16[1024,256]{1,0:T(8,128)(2,1)S(1)} %backward.10), kind=kLoop, calls=%fused_computation.4 | loop fusion | flops 1572864 | bytes 2097152 | tf_op jit(solution)/shard_map/convert_element_type | solution.py:383
  192.2 1.3 collective-permute-done.25
  194.8 4.6 %copy-done.6 = bf16[32,1,12,128,128]{4,3,2,1,0:T(8,128)(2,1)S(1)} copy-done((bf16[32,1,12,128,128]{4,3,2,1,0:T(8,128)(2,1)S(1)}, bf16[32,1,12,128,128]{4,3,2,1,0:T(8,128)(2,1)}, u32[]{:S(2)}) %copy-start.6) | copy-done | bytes 12582936
  199.4 2.1 %backward.8 = bf16[1024,256]{1,0:T(8,128)(2,1)S(1)} custom-call(s32[64]{0:T(128)S(1)} %copy-done.10, s32[2304]{0:T(1024)S(1)} %copy-done.7, s32[2304]{0:T(1024)S(1)} %copy-done.8, bf16[384,128,128]{2,1,0:T(8,128)(2,1)S(1)} %bitcast.44, bf16[1024,256]{1,0:T(8,128)(2,1)S(1)} %convolution_convert_fusion.refs_0_, ...), custom_call_target="tpu_custom_call" | custom-call | flops 402653184 | bytes 4194304 | tf_op jit(solution)/shard_map/backward/pallas_call | solution.py:252
  201.5 4.6 %collective-permute-done.18 = bf16[1024,256]{1,0:T(8,128)(2,1)} collective-permute-done((bf16[1024,256]{1,0:T(8,128)(2,1)}, bf16[1024,256]{1,0:T(8,128)(2,1)}, u32[]{:S(2)}, u32[]{:S(2)}) %collective-permute-start.18) | collective-permute-done | bytes 524320 | tf_op jit(solution)/shard_map/ppermute | solution.py:385
  206.1 2.2 %add_convert_fusion = bf16[1024,256]{1,0:T(8,128)(2,1)} fusion(bf16[1024,256]{1,0:T(8,128)(2,1)} %collective-permute-done.18, bf16[1024,256]{1,0:T(8,128)(2,1)} %collective-permute-done.12, bf16[1024,256]{1,0:T(8,128)(2,1)S(1)} %backward.8), kind=kLoop, calls=%fused_computation.3 | loop fusion | flops 1572864 | bytes 2097152 | tf_op jit(solution)/shard_map/convert_element_type | solution.py:383
  (93 shorter events, 10.9 us)
Async XLA Ops:
  0.6 93.6 %copy-start = (bf16[256,256]{1,0:T(8,128)(2,1)S(1)}, bf16[256,256]{1,0:T(8,128)(2,1)}, u32[]{:S(2)}) copy-start(bf16[256,256]{1,0:T(8,128)(2,1)} %param.11) | copy-start | bytes 393220
  0.6 17.3 %collective-permute-start = (bf16[1024,256]{1,0:T(8,128)(2,1)}, bf16[1024,256]{1,0:T(8,128)(2,1)S(1)}, u32[]{:S(2)}, u32[]{:S(2)}) collective-permute-start(bf16[1024,256]{1,0:T(8,128)(2,1)} %refs_0_.1), channel_id=1, source_target_pairs={{0,8},{4,12},{8,16},{12,20},{16,24},{20,28},{24,0},{28,4},{1,9},{5... | collective-permute-start | bytes 1572872 | tf_op jit(solution)/shard_map/ppermute | solution.py:310
  17.9 14.9 %collective-permute-start.1 = (bf16[1024,256]{1,0:T(8,128)(2,1)S(1)}, bf16[1024,256]{1,0:T(8,128)(2,1)S(1)}, u32[]{:S(2)}, u32[]{:S(2)}) collective-permute-start(bf16[1024,256]{1,0:T(8,128)(2,1)S(1)} %collective-permute-done.refs_2_), channel_id=1, source_target_pairs={{0,8},{4,12},{8,16},{12,20},{16,24},{20,28},{24,0},{28,4},{1,9},{5... | collective-permute-start | bytes 1572872 | tf_op jit(solution)/shard_map/ppermute | solution.py:310
  17.9 35.1 %collective-permute-start.4 = (bf16[1024,256]{1,0:T(8,128)(2,1)}, bf16[1024,256]{1,0:T(8,128)(2,1)S(1)}, u32[]{:S(2)}, u32[]{:S(2)}) collective-permute-start(bf16[1024,256]{1,0:T(8,128)(2,1)} %refs_0_.1), channel_id=1, source_target_pairs={{0,4},{4,0},{8,12},{12,8},{16,20},{20,16},{24,28},{28,24},{1,5},{5... | collective-permute-start | bytes 1572872 | tf_op jit(solution)/shard_map/ppermute | solution.py:307
  32.8 14.0 %collective-permute-start.2 = (bf16[1024,256]{1,0:T(8,128)(2,1)S(1)}, bf16[1024,256]{1,0:T(8,128)(2,1)S(1)}, u32[]{:S(2)}, u32[]{:S(2)}) collective-permute-start(bf16[1024,256]{1,0:T(8,128)(2,1)S(1)} %collective-permute-done.1.refs_4_), channel_id=1, source_target_pairs={{0,8},{4,12},{8,16},{12,20},{16,24},{20,28},{24,0},{28,4},{1,9},{5... | collective-permute-start | bytes 1572872 | tf_op jit(solution)/shard_map/ppermute | solution.py:310
  34.6 18.4 %collective-permute-start.5 = (bf16[1024,256]{1,0:T(8,128)(2,1)S(1)}, bf16[1024,256]{1,0:T(8,128)(2,1)S(1)}, u32[]{:S(2)}, u32[]{:S(2)}) collective-permute-start(bf16[1024,256]{1,0:T(8,128)(2,1)S(1)} %collective-permute-done.refs_2_), channel_id=1, source_target_pairs={{0,4},{4,0},{8,12},{12,8},{16,20},{20,16},{24,28},{28,24},{1,5},{5... | collective-permute-start | bytes 1572872 | tf_op jit(solution)/shard_map/ppermute | solution.py:307
  35.9 24.9 %collective-permute-start.6 = (bf16[1024,256]{1,0:T(8,128)(2,1)S(1)}, bf16[1024,256]{1,0:T(8,128)(2,1)}, u32[]{:S(2)}, u32[]{:S(2)}) collective-permute-start(bf16[1024,256]{1,0:T(8,128)(2,1)S(1)} %collective-permute-done.1.refs_4_), channel_id=1, source_target_pairs={{0,4},{4,0},{8,12},{12,8},{16,20},{20,16},{24,28},{28,24},{1,5},{5... | collective-permute-start | bytes 1572872 | tf_op jit(solution)/shard_map/ppermute | solution.py:307
  46.8 27.7 %collective-permute-start.3 = (bf16[1024,256]{1,0:T(8,128)(2,1)S(1)}, bf16[1024,256]{1,0:T(8,128)(2,1)S(1)}, u32[]{:S(2)}, u32[]{:S(2)}) collective-permute-start(bf16[1024,256]{1,0:T(8,128)(2,1)S(1)} %collective-permute-done.2.refs_6_), channel_id=1, source_target_pairs={{0,4},{4,0},{8,12},{12,8},{16,20},{20,16},{24,28},{28,24},{1,5},{5... | collective-permute-start | bytes 1572872 | tf_op jit(solution)/shard_map/ppermute | solution.py:307
  60.7 4.6 %copy-start.1 = (bf16[32,1,12,128,128]{4,3,2,1,0:T(8,128)(2,1)S(1)}, bf16[32,1,12,128,128]{4,3,2,1,0:T(8,128)(2,1)}, u32[]{:S(2)}) copy-start(bf16[32,1,12,128,128]{4,3,2,1,0:T(8,128)(2,1)} %param.8) | copy-start | bytes 37748740
  65.3 1.0 copy-start.9
  66.4 8.1 %copy-start.2 = (bf16[32,1,12,128,128]{4,3,2,1,0:T(8,128)(2,1)S(1)}, bf16[32,1,12,128,128]{4,3,2,1,0:T(8,128)(2,1)}, u32[]{:S(2)}) copy-start(bf16[32,1,12,128,128]{4,3,2,1,0:T(8,128)(2,1)} %param.8) | copy-start | bytes 37748740
  66.4 8.2 %copy-start.11 = (s32[448]{0:T(512)S(1)}, s32[448]{0:T(512)}, u32[]{:S(2)}) copy-start(s32[448]{0:T(512)} %get-tuple-element.13.entry_ref) | copy-start | bytes 5380
  66.4 8.2 %copy-start.12 = (s32[448]{0:T(512)S(1)}, s32[448]{0:T(512)}, u32[]{:S(2)}) copy-start(s32[448]{0:T(512)} %get-tuple-element.14.source_ref) | copy-start | bytes 5380
  66.4 8.2 %copy-start.13 = (s32[32]{0:T(128)S(1)}, s32[32]{0:T(128)}, u32[]{:S(2)}) copy-start(s32[32]{0:T(128)} %get-tuple-element.12.count_ref) | copy-start | bytes 388
  77.0 2.7 %collective-permute-start.7 = (bf16[2048,256]{1,0:T(8,128)(2,1)S(1)}, bf16[2048,256]{1,0:T(8,128)(2,1)S(1)}, u32[]{:S(2)}, u32[]{:S(2)}) collective-permute-start(bf16[2048,256]{1,0:T(8,128)(2,1)S(1)} %late.3), channel_id=1, source_target_pairs={{0,1},{1,0},{2,3},{3,2},{4,5},{5,4},{6,7},{7,6},{8,9},{9,8},{10,11... | collective-permute-start | bytes 3145736 | tf_op jit(solution)/shard_map/ppermute | solution.py:324
  77.1 17.2 %copy-start.18 = (bf16[1024,256]{1,0:T(8,128)(2,1)S(1)}, bf16[1024,256]{1,0:T(8,128)(2,1)}, u32[]{:S(2)}) copy-start(bf16[1024,256]{1,0:T(8,128)(2,1)} %param.13) | copy-start | bytes 1572868
  77.1 17.2 %copy-start.21 = (f32[256]{0:T(256)S(1)}, f32[256]{0:T(256)}, u32[]{:S(2)}) copy-start(f32[256]{0:T(256)} %param.12) | copy-start | bytes 3076
  79.7 16.1 %copy-start.16 = (bf16[2048,256]{1,0:T(8,128)(2,1)}, bf16[2048,256]{1,0:T(8,128)(2,1)S(1)}, u32[]{:S(2)}) copy-start(bf16[2048,256]{1,0:T(8,128)(2,1)S(1)} %collective-permute-done.7) | copy-start | bytes 3145732
  79.9 32.5 %copy-start.7 = (s32[2304]{0:T(1024)S(1)}, s32[2304]{0:T(1024)}, u32[]{:S(2)}) copy-start(s32[2304]{0:T(1024)} %get-tuple-element.18.entry_ref) | copy-start | bytes 27652
  79.9 32.5 %copy-start.8 = (s32[2304]{0:T(1024)S(1)}, s32[2304]{0:T(1024)}, u32[]{:S(2)}) copy-start(s32[2304]{0:T(1024)} %get-tuple-element.19.source_ref) | copy-start | bytes 27652
  79.9 32.4 %copy-start.10 = (s32[64]{0:T(128)S(1)}, s32[64]{0:T(128)}, u32[]{:S(2)}) copy-start(s32[64]{0:T(128)} %get-tuple-element.17.count_ref) | copy-start | bytes 772
  79.9 14.3 %collective-permute-start.8 = (bf16[1024,256]{1,0:T(8,128)(2,1)S(1)}, bf16[1024,256]{1,0:T(8,128)(2,1)S(1)}, u32[]{:S(2)}, u32[]{:S(2)}) collective-permute-start(bf16[1024,256]{1,0:T(8,128)(2,1)S(1)} %add_convert_fusion.5), channel_id=1, source_target_pairs={{0,2},{1,3},{2,0},{3,1},{4,6},{5,7},{6,4},{7,5},{8,10},{9,11},{10,... | collective-permute-start | bytes 1572872 | tf_op jit(solution)/shard_map/ppermute | solution.py:334
  94.2 1.5 copy-start.19
  95.8 0.8 copy-start.14
  96.9 13.5 %collective-permute-start.10 = (bf16[1024,256]{1,0:T(8,128)(2,1)S(1)}, bf16[1024,256]{1,0:T(8,128)(2,1)S(1)}, u32[]{:S(2)}, u32[]{:S(2)}) collective-permute-start(bf16[1024,256]{1,0:T(8,128)(2,1)S(1)} %convolution_convert_fusion.refs_0_), channel_id=1, source_target_pairs={{0,2},{1,3},{2,0},{3,1},{4,6},{5,7},{6,4},{7,5},{8,10},{9,11},{10,... | collective-permute-start | bytes 1572872 | tf_op jit(solution)/shard_map/ppermute | solution.py:356
  98.3 12.1 %collective-permute-start.9 = (bf16[1024,256]{1,0:T(8,128)(2,1)S(1)}, bf16[1024,256]{1,0:T(8,128)(2,1)S(1)}, u32[]{:S(2)}, u32[]{:S(2)}) collective-permute-start(bf16[1024,256]{1,0:T(8,128)(2,1)S(1)} %convolution_convert_fusion.refs_0_), channel_id=1, source_target_pairs={{0,1},{1,0},{2,3},{3,2},{4,5},{5,4},{6,7},{7,6},{8,9},{9,8},{10,11... | collective-permute-start | bytes 1572872 | tf_op jit(solution)/shard_map/ppermute | solution.py:353
  110.4 1.9 collective-permute-start.11
  112.3 4.6 %copy-start.3 = (bf16[32,1,12,128,128]{4,3,2,1,0:T(8,128)(2,1)S(1)}, bf16[32,1,12,128,128]{4,3,2,1,0:T(8,128)(2,1)}, u32[]{:S(2)}) copy-start(bf16[32,1,12,128,128]{4,3,2,1,0:T(8,128)(2,1)} %param.8) | copy-start | bytes 37748740
  116.9 3.6 %copy-start.15 = (bf16[1024,256]{1,0:T(8,128)(2,1)S(1)}, bf16[1024,256]{1,0:T(8,128)(2,1)}, u32[]{:S(2)}) copy-start(bf16[1024,256]{1,0:T(8,128)(2,1)} %copy-done.14) | copy-start | bytes 1572868
  116.9 3.6 %copy-start.17 = (bf16[2048,256]{1,0:T(8,128)(2,1)S(1)}, bf16[2048,256]{1,0:T(8,128)(2,1)}, u32[]{:S(2)}) copy-start(bf16[2048,256]{1,0:T(8,128)(2,1)} %copy-done.16) | copy-start | bytes 3145732
  116.9 3.6 %copy-start.20 = (bf16[1024,256]{1,0:T(8,128)(2,1)S(1)}, bf16[1024,256]{1,0:T(8,128)(2,1)}, u32[]{:S(2)}) copy-start(bf16[1024,256]{1,0:T(8,128)(2,1)} %copy-done.19) | copy-start | bytes 1572868
  119.1 14.9 %collective-permute-start.15 = (bf16[1024,256]{1,0:T(8,128)(2,1)S(1)}, bf16[1024,256]{1,0:T(8,128)(2,1)S(1)}, u32[]{:S(2)}, u32[]{:S(2)}) collective-permute-start(bf16[1024,256]{1,0:T(8,128)(2,1)S(1)} %backward.15), channel_id=1, source_target_pairs={{0,4},{4,0},{8,12},{12,8},{16,20},{20,16},{24,28},{28,24},{1,5},{5... | collective-permute-start | bytes 1572872 | tf_op jit(solution)/shard_map/ppermute | solution.py:377
  121.0 13.9 %collective-permute-start.19 = (f32[144,256]{1,0:T(8,128)S(1)}, f32[144,256]{1,0:T(8,128)S(1)}, u32[]{:S(2)}, u32[]{:S(2)}) collective-permute-start(f32[144,256]{1,0:T(8,128)S(1)} %dynamic-slice_bitcast_fusion), channel_id=1, source_target_pairs={{0,1},{1,0},{2,3},{3,2},{4,5},{5,4},{6,7},{7,6},{8,9},{9,8},{10,11... | collective-permute-start | bytes 442376 | tf_op jit(solution)/shard_map/ppermute | solution.py:404
  123.2 28.1 %collective-permute-start.14 = (bf16[1024,256]{1,0:T(8,128)(2,1)S(1)}, bf16[1024,256]{1,0:T(8,128)(2,1)}, u32[]{:S(2)}, u32[]{:S(2)}) collective-permute-start(bf16[1024,256]{1,0:T(8,128)(2,1)S(1)} %backward.13), channel_id=1, source_target_pairs={{0,4},{4,0},{8,12},{12,8},{16,20},{20,16},{24,28},{28,24},{1,5},{5... | collective-permute-start | bytes 1572872 | tf_op jit(solution)/shard_map/ppermute | solution.py:377
  134.9 16.4 %collective-permute-start.16 = (bf16[1024,256]{1,0:T(8,128)(2,1)}, bf16[1024,256]{1,0:T(8,128)(2,1)}, u32[]{:S(2)}, u32[]{:S(2)}) collective-permute-start(bf16[1024,256]{1,0:T(8,128)(2,1)} %add_convert_fusion.3), channel_id=1, source_target_pairs={{0,8},{4,12},{8,16},{12,20},{16,24},{20,28},{24,0},{28,4},{1,9},{5... | collective-permute-start | bytes 1572872 | tf_op jit(solution)/shard_map/ppermute | solution.py:385
  134.9 4.7 %collective-permute-start.20 = (f32[72,256]{1,0:T(8,128)S(1)}, f32[72,256]{1,0:T(8,128)S(1)}, u32[]{:S(2)}, u32[]{:S(2)}) collective-permute-start(f32[72,256]{1,0:T(8,128)S(1)} %dynamic-slice_bitcast_fusion.1), channel_id=1, source_target_pairs={{0,2},{1,3},{2,0},{3,1},{4,6},{5,7},{6,4},{7,5},{8,10},{9,11},{10,... | collective-permute-start | bytes 221192 | tf_op jit(solution)/shard_map/ppermute | solution.py:404
  139.6 15.0 %collective-permute-start.21 = (f32[72,256]{1,0:T(8,128)S(1)}, f32[72,256]{1,0:T(8,128)S(1)}, u32[]{:S(2)}, u32[]{:S(2)}) collective-permute-start(f32[72,256]{1,0:T(8,128)S(1)} %bitcast_add_fusion.1), channel_id=1, source_target_pairs={{0,4},{4,0},{8,12},{12,8},{16,20},{20,16},{24,28},{28,24},{1,5},{5... | collective-permute-start | bytes 221192 | tf_op jit(solution)/shard_map/ppermute | solution.py:419
  141.4 4.6 %copy-start.4 = (bf16[32,1,12,128,128]{4,3,2,1,0:T(8,128)(2,1)S(1)}, bf16[32,1,12,128,128]{4,3,2,1,0:T(8,128)(2,1)}, u32[]{:S(2)}) copy-start(bf16[32,1,12,128,128]{4,3,2,1,0:T(8,128)(2,1)} %param.8) | copy-start | bytes 37748740
  148.4 41.4 %collective-permute-start.13 = (bf16[1024,256]{1,0:T(8,128)(2,1)S(1)}, bf16[1024,256]{1,0:T(8,128)(2,1)}, u32[]{:S(2)}, u32[]{:S(2)}) collective-permute-start(bf16[1024,256]{1,0:T(8,128)(2,1)S(1)} %backward.11), channel_id=1, source_target_pairs={{0,4},{4,0},{8,12},{12,8},{16,20},{20,16},{24,28},{28,24},{1,5},{5... | collective-permute-start | bytes 1572872 | tf_op jit(solution)/shard_map/ppermute | solution.py:377
  153.5 36.3 %collective-permute-start.17 = (bf16[1024,256]{1,0:T(8,128)(2,1)}, bf16[1024,256]{1,0:T(8,128)(2,1)}, u32[]{:S(2)}, u32[]{:S(2)}) collective-permute-start(bf16[1024,256]{1,0:T(8,128)(2,1)} %add_convert_fusion.2), channel_id=1, source_target_pairs={{0,8},{4,12},{8,16},{12,20},{16,24},{20,28},{24,0},{28,4},{1,9},{5... | collective-permute-start | bytes 1572872 | tf_op jit(solution)/shard_map/ppermute | solution.py:385
  154.6 14.4 %collective-permute-start.22 = (f32[72,256]{1,0:T(8,128)S(1)}, f32[72,256]{1,0:T(8,128)S(1)}, u32[]{:S(2)}, u32[]{:S(2)}) collective-permute-start(f32[72,256]{1,0:T(8,128)S(1)} %add.270), channel_id=1, source_target_pairs={{0,8},{4,12},{8,0},{12,4},{16,24},{20,28},{24,16},{28,20},{1,9},{5... | collective-permute-start | bytes 221192 | tf_op jit(solution)/shard_map/ppermute | solution.py:419
  169.1 5.9 %collective-permute-start.23 = (f32[72,256]{1,0:T(8,128)S(1)}, f32[72,256]{1,0:T(8,128)S(1)}, u32[]{:S(2)}, u32[]{:S(2)}) collective-permute-start(f32[72,256]{1,0:T(8,128)S(1)} %add.271), channel_id=1, source_target_pairs={{0,16},{4,20},{8,24},{12,28},{16,0},{20,4},{24,8},{28,12},{1,17},{... | collective-permute-start | bytes 221192 | tf_op jit(solution)/shard_map/ppermute | solution.py:419
  175.0 17.0 %collective-permute-start.24 = (f32[72,256]{1,0:T(8,128)S(1)}, f32[72,256]{1,0:T(8,128)S(1)}, u32[]{:S(2)}, u32[]{:S(2)}) collective-permute-start(f32[72,256]{1,0:T(8,128)S(1)} %get-tuple-element.21), channel_id=1, source_target_pairs={{0,2},{1,3},{2,0},{3,1},{4,6},{5,7},{6,4},{7,5},{8,10},{9,11},{10,... | collective-permute-start | bytes 221192 | tf_op jit(solution)/shard_map/ppermute | solution.py:412
  178.7 4.6 %copy-start.5 = (bf16[32,1,12,128,128]{4,3,2,1,0:T(8,128)(2,1)S(1)}, bf16[32,1,12,128,128]{4,3,2,1,0:T(8,128)(2,1)}, u32[]{:S(2)}) copy-start(bf16[32,1,12,128,128]{4,3,2,1,0:T(8,128)(2,1)} %param.8) | copy-start | bytes 37748740
  185.7 15.8 %collective-permute-start.12 = (bf16[1024,256]{1,0:T(8,128)(2,1)S(1)}, bf16[1024,256]{1,0:T(8,128)(2,1)}, u32[]{:S(2)}, u32[]{:S(2)}) collective-permute-start(bf16[1024,256]{1,0:T(8,128)(2,1)S(1)} %backward.9), channel_id=1, source_target_pairs={{0,4},{4,0},{8,12},{12,8},{16,20},{20,16},{24,28},{28,24},{1,5},{5... | collective-permute-start | bytes 1572872 | tf_op jit(solution)/shard_map/ppermute | solution.py:377
  192.0 14.1 %collective-permute-start.18 = (bf16[1024,256]{1,0:T(8,128)(2,1)}, bf16[1024,256]{1,0:T(8,128)(2,1)}, u32[]{:S(2)}, u32[]{:S(2)}) collective-permute-start(bf16[1024,256]{1,0:T(8,128)(2,1)} %add_convert_fusion.1), channel_id=1, source_target_pairs={{0,8},{4,12},{8,16},{12,20},{16,24},{20,28},{24,0},{28,4},{1,9},{5... | collective-permute-start | bytes 1572872 | tf_op jit(solution)/shard_map/ppermute | solution.py:385
  192.1 1.4 collective-permute-start.25
  194.8 4.6 %copy-start.6 = (bf16[32,1,12,128,128]{4,3,2,1,0:T(8,128)(2,1)S(1)}, bf16[32,1,12,128,128]{4,3,2,1,0:T(8,128)(2,1)}, u32[]{:S(2)}) copy-start(bf16[32,1,12,128,128]{4,3,2,1,0:T(8,128)(2,1)} %param.8) | copy-start | bytes 37748740
